TPU v7x, 32 devices: a whole 2x2x4 slice. The times are simulated.
32 devices in a mesh: clip: 16 (over z, x, core), frame: 2 (over y).
Axes of the slice: x: 2, y: 2, z: 4, core: 2. Of those that a mesh axis runs over, the one named last changes fastest.
Arguments:
- inputs: bfloat16 [16, 1500, 768], P('clip', 'frame'), may hold values from -6 to 6
- cotangent: bfloat16 [16, 1500, 768], P('clip', 'frame'), may hold values from -2 to 2
- project_in: float32 [768, 2304], P(('clip', 'frame'))
- project_out: float32 [768, 768], P(('clip', 'frame')), may hold values from -0.1875 to 0.1875
- expand_weight: float32 [768, 3072], P(('clip', 'frame')), may hold values from -0.21875 to 0.21875
- shrink_weight: float32 [3072, 768], P(('clip', 'frame')), may hold values from -0.15625 to 0.15625
- expand_bias: float32 [3072], P(('clip', 'frame')), may hold values from -3 to 3
- vectors: float32 [768, 8], P(('clip', 'frame'))
- moments_in: float32 [2, 768, 2304], P(None, ('clip', 'frame')), as said below
- moments_out: float32 [2, 768, 768], P(None, ('clip', 'frame'))
- moments_expand: float32 [2, 768, 3072], P(None, ('clip', 'frame'))
- moments_shrink: float32 [2, 3072, 768], P(None, ('clip', 'frame'))
- moments_bias: float32 [2, 3072], P(None, ('clip', 'frame'))
- moments_vectors: float32 [2, 768, 8], P(None, ('clip', 'frame'))
Outputs:
- output: bfloat16 [16, 1500, 768], P('clip', 'frame')
- grad_inputs: bfloat16 [16, 1500, 768], P('clip', 'frame')
- grad_project_in: float32 [768, 2304], P(('clip', 'frame'))
- grad_project_out: float32 [768, 768], P(('clip', 'frame'))
- grad_expand: float32 [768, 3072], P(('clip', 'frame'))
- grad_shrink: float32 [3072, 768], P(('clip', 'frame'))
- grad_bias: float32 [3072], P(('clip', 'frame'))
- grad_vectors: float32 [768, 8], P(('clip', 'frame'))
- new_project_in: float32 [768, 2304], P(('clip', 'frame'))
- new_project_out: float32 [768, 768], P(('clip', 'frame'))
- new_expand: float32 [768, 3072], P(('clip', 'frame'))
- new_shrink: float32 [3072, 768], P(('clip', 'frame'))
- new_bias: float32 [3072], P(('clip', 'frame'))
- new_vectors: float32 [768, 8], P(('clip', 'frame'))
- new_moments_in: float32 [2, 768, 2304], P(None, ('clip', 'frame'))
- new_moments_out: float32 [2, 768, 768], P(None, ('clip', 'frame'))
- new_moments_expand: float32 [2, 768, 3072], P(None, ('clip', 'frame'))
- new_moments_shrink: float32 [2, 3072, 768], P(None, ('clip', 'frame'))
- new_moments_bias: float32 [2, 3072], P(None, ('clip', 'frame'))
- new_moments_vectors: float32 [2, 768, 8], P(None, ('clip', 'frame'))
Inputs may be any that keep to these rules, and one draw needn't show every extreme that they name: `moments_in`: the first row of each moments array is signed, the second positive.
All inputs are finite; a program needn't handle non-finite values.
Results may differ from a plain program's by a relative error of at most 0.013.
The roundings to bfloat16 on the way count: a program that leaves them out, or rounds other values in their place, can miss the bound.
Values may be sent and summed in bfloat16 or wider, within the bound.
A program may use at most 192 MiB of HBM per device.

v0:
```python
import math
import jax
import jax.numpy as jnp
from jax import lax
from jax.sharding import PartitionSpec as P

HEADS = 12
ADAM_STEP = 4
epsilon_norm = 1e-05
beta_first = 0.9
beta_second = 0.99
learn_rate = 0.03
decay_rate = 0.01
epsilon_adam = 1e-08
root_half = 0.7071067811865476
inv_root_two_pi = 0.3989422804014327


def norm_parts(inputs, norm_gain, norm_shift):
    average = jnp.mean(inputs, axis=-1, keepdims=True)
    centered = inputs - average
    spread = jnp.mean(centered * centered, axis=-1, keepdims=True)
    inv_std = lax.rsqrt(spread + epsilon_norm)
    normed = centered * inv_std
    return (normed * norm_gain + norm_shift, normed, inv_std)


def norm_backward(grad_normed, normed, inv_std, norm_gain):
    grad_gain = jnp.sum(grad_normed * normed, axis=0)
    grad_shift = jnp.sum(grad_normed, axis=0)
    scaled = grad_normed * norm_gain
    grad_input = inv_std * (
        scaled
        - jnp.mean(scaled, axis=-1, keepdims=True)
        - normed * jnp.mean(scaled * normed, axis=-1, keepdims=True)
    )
    return (grad_input, grad_gain, grad_shift)


def gelu_exact(inputs):
    return 0.5 * inputs * (1.0 + jax.scipy.special.erf(inputs * root_half))


def gelu_slope(inputs):
    return (
        0.5 * (1.0 + jax.scipy.special.erf(inputs * root_half))
        + inputs * jnp.exp(-0.5 * inputs * inputs) * inv_root_two_pi
    )


def attend_forward(queries, keys_values, head_count):
    model_width = queries.shape[2]
    head_size = model_width // head_count
    score_scale = 1.0 / math.sqrt(head_size)

    def one_head(head_index):
        offset = head_index * head_size
        query_block = lax.dynamic_slice_in_dim(queries, offset, head_size, 2)
        key_block = lax.dynamic_slice_in_dim(keys_values, offset, head_size, 2)
        value_block = lax.dynamic_slice_in_dim(keys_values, model_width + offset, head_size, 2)
        scores = (
            jnp.einsum("cqd,ckd->cqk", query_block, key_block, preferred_element_type=jnp.float32)
            * score_scale
        )
        highest = jnp.max(scores, axis=-1, keepdims=True)
        exponent = jnp.exp(scores - highest)
        denominator = jnp.sum(exponent, axis=-1, keepdims=True)
        weights_soft = (exponent / denominator).astype(jnp.bfloat16)
        mixed = jnp.einsum(
            "cqk,ckd->cqd", weights_soft, value_block, preferred_element_type=jnp.float32
        )
        return (mixed, (highest + jnp.log(denominator))[..., 0])

    mixed, log_totals = lax.map(one_head, jnp.arange(head_count))
    clip_count, frame_count = (queries.shape[0], queries.shape[1])
    mixed = jnp.transpose(mixed, (1, 2, 0, 3)).reshape(clip_count, frame_count, model_width)
    return (mixed, log_totals)


def attend_backward(queries, keys_values, grad_mixed, log_totals, head_count):
    model_width = queries.shape[2]
    head_size = model_width // head_count
    score_scale = 1.0 / math.sqrt(head_size)

    def one_head_back(head_index):
        offset = head_index * head_size
        query_block = lax.dynamic_slice_in_dim(queries, offset, head_size, 2)
        key_block = lax.dynamic_slice_in_dim(keys_values, offset, head_size, 2)
        value_block = lax.dynamic_slice_in_dim(keys_values, model_width + offset, head_size, 2)
        grad_block = lax.dynamic_slice_in_dim(grad_mixed, offset, head_size, 2)
        totals = lax.dynamic_index_in_dim(log_totals, head_index, 0, keepdims=False)
        scores = (
            jnp.einsum("cqd,ckd->cqk", query_block, key_block, preferred_element_type=jnp.float32)
            * score_scale
        )
        weights_soft = jnp.exp(scores - totals[..., None])
        grad_weights = jnp.einsum(
            "cqd,ckd->cqk", grad_block, value_block, preferred_element_type=jnp.float32
        )
        delta = jnp.sum(weights_soft * grad_weights, axis=-1, keepdims=True)
        grad_scores = (weights_soft * (grad_weights - delta)).astype(jnp.bfloat16)
        grad_query = (
            jnp.einsum("cqk,ckd->cqd", grad_scores, key_block, preferred_element_type=jnp.float32)
            * score_scale
        )
        grad_key = (
            jnp.einsum("cqk,cqd->ckd", grad_scores, query_block, preferred_element_type=jnp.float32)
            * score_scale
        )
        grad_value = jnp.einsum(
            "cqk,cqd->ckd",
            weights_soft.astype(jnp.bfloat16),
            grad_block,
            preferred_element_type=jnp.float32,
        )
        return (grad_query, delta[..., 0], grad_key, grad_value)

    pieces = lax.map(one_head_back, jnp.arange(head_count))
    clip_count, frame_count = (queries.shape[0], queries.shape[1])
    clip_frames = keys_values.shape[1]
    grad_query = jnp.transpose(pieces[0], (1, 2, 0, 3)).reshape(
        clip_count, frame_count, model_width
    )
    grad_key = jnp.transpose(pieces[2], (1, 2, 0, 3)).reshape(clip_count, clip_frames, model_width)
    grad_value = jnp.transpose(pieces[3], (1, 2, 0, 3)).reshape(
        clip_count, clip_frames, model_width
    )
    return (grad_query, pieces[1], jnp.concatenate([grad_key, grad_value], axis=2))


def adam_step(weight, moments, gradient):
    first = beta_first * moments[0] + (1.0 - beta_first) * gradient
    second = beta_second * moments[1] + (1.0 - beta_second) * gradient * gradient
    first_hat = first / (1.0 - beta_first**ADAM_STEP)
    second_hat = second / (1.0 - beta_second**ADAM_STEP)
    change = -learn_rate * (first_hat / (jnp.sqrt(second_hat) + epsilon_adam) + decay_rate * weight)
    return (change, jnp.stack([first, second]))


def body(
    inputs,
    cotangent,
    project_in,
    project_out,
    expand_weight,
    shrink_weight,
    expand_bias,
    vectors,
    moments_in,
    moments_out,
    moments_expand,
    moments_shrink,
    moments_bias,
    moments_vectors,
):
    clip_count, frame_count, model_width = inputs.shape
    row_count = clip_count * frame_count
    head_count = HEADS
    shard_rows = project_in.shape[0]
    wide_in = project_in.shape[1]
    ff_width = expand_weight.shape[1]
    swap = [(0, 1), (1, 0)]
    everyone = ("clip", "frame")
    small = jnp.concatenate(
        [
            vectors,
            expand_bias.reshape(shard_rows, -1),
            jnp.zeros(
                (shard_rows, 128 - vectors.shape[1] - expand_bias.shape[0] // shard_rows),
                jnp.float32,
            ),
        ],
        axis=1,
    )
    first_pack = jnp.concatenate([project_in, small], axis=1).astype(jnp.bfloat16)
    second_pack = jnp.concatenate(
        [project_out, expand_weight, shrink_weight.reshape(shard_rows, -1)], axis=1
    ).astype(jnp.bfloat16)
    first_full = lax.all_gather(first_pack, everyone, axis=0, tiled=True)
    second_full = lax.all_gather(second_pack, everyone, axis=0, tiled=True)
    full_in = first_full[:, :wide_in]
    small_full = first_full[:, wide_in:].astype(jnp.float32)
    column_set = small_full[:, : vectors.shape[1]]
    full_bias = small_full[
        :, vectors.shape[1] : vectors.shape[1] + ff_width // model_width
    ].reshape(-1)
    full_out = second_full[:, :model_width]
    full_expand = second_full[:, model_width : model_width + ff_width]
    full_shrink = second_full[:, model_width + ff_width :].reshape(ff_width, model_width)
    frames_rows = inputs.reshape(row_count, model_width).astype(jnp.float32)
    normed_first, plain_first, inv_first = norm_parts(
        frames_rows, column_set[:, 0], column_set[:, 1]
    )
    hidden_first = normed_first.astype(jnp.bfloat16)
    hidden_partner = lax.ppermute(hidden_first, "frame", swap)
    bias_in = jnp.concatenate(
        [column_set[:, 2], jnp.zeros((model_width,), jnp.float32), column_set[:, 3]]
    )
    projected = (
        jnp.dot(hidden_first, full_in, preferred_element_type=jnp.float32) + bias_in
    ).astype(jnp.bfloat16)
    partner_pairs = (
        jnp.dot(hidden_partner, full_in[:, model_width:], preferred_element_type=jnp.float32)
        + bias_in[model_width:]
    ).astype(jnp.bfloat16)
    queries = projected[:, :model_width].reshape(clip_count, frame_count, model_width)
    clip_pairs = jnp.concatenate([projected[:, model_width:], partner_pairs], axis=0).reshape(
        clip_count, 2 * frame_count, 2 * model_width
    )
    mixed, log_totals = attend_forward(queries, clip_pairs, head_count)
    mixed_low = mixed.reshape(row_count, model_width).astype(jnp.bfloat16)
    attended = jnp.dot(mixed_low, full_out, preferred_element_type=jnp.float32) + column_set[:, 4]
    residual = frames_rows + attended
    normed_second, plain_second, inv_second = norm_parts(
        residual, column_set[:, 5], column_set[:, 6]
    )
    hidden_second = normed_second.astype(jnp.bfloat16)
    preact = jnp.dot(hidden_second, full_expand, preferred_element_type=jnp.float32) + full_bias
    activated = gelu_exact(preact).astype(jnp.bfloat16)
    result = (
        residual
        + jnp.dot(activated, full_shrink, preferred_element_type=jnp.float32)
        + column_set[:, 7]
    )
    output = result.astype(jnp.bfloat16).reshape(inputs.shape)
    grad_result = cotangent.reshape(row_count, model_width)
    grad_shrink_term = jnp.dot(activated.T, grad_result, preferred_element_type=jnp.float32)
    grad_down_bias = jnp.sum(grad_result.astype(jnp.float32), axis=0)
    grad_activated = jnp.dot(grad_result, full_shrink.T, preferred_element_type=jnp.float32)
    grad_preact = (grad_activated * gelu_slope(preact)).astype(jnp.bfloat16)
    grad_expand_term = jnp.dot(hidden_second.T, grad_preact, preferred_element_type=jnp.float32)
    grad_bias_term = jnp.sum(grad_preact.astype(jnp.float32), axis=0)
    grad_hidden_second = jnp.dot(grad_preact, full_expand.T, preferred_element_type=jnp.float32)
    norm_term_second, gain_second, shift_second = norm_backward(
        grad_hidden_second, plain_second, inv_second, column_set[:, 5]
    )
    grad_residual = grad_result.astype(jnp.float32) + norm_term_second
    grad_attended = grad_residual.astype(jnp.bfloat16)
    grad_out_term = jnp.dot(mixed_low.T, grad_attended, preferred_element_type=jnp.float32)
    grad_out_bias = jnp.sum(grad_attended.astype(jnp.float32), axis=0)
    owned_late = lax.psum_scatter(
        jnp.concatenate(
            [grad_shrink_term.reshape(model_width, -1), grad_expand_term, grad_out_term], axis=1
        ),
        everyone,
        scatter_dimension=0,
        tiled=True,
    )
    grad_mixed = jnp.dot(grad_attended, full_out.T, preferred_element_type=jnp.float32).astype(
        jnp.bfloat16
    )
    grad_mixed = grad_mixed.reshape(clip_count, frame_count, model_width)
    grad_query, delta_rows, grad_pairs_terms = attend_backward(
        queries, clip_pairs, grad_mixed, log_totals, head_count
    )
    partner_terms = grad_pairs_terms[:, frame_count:].astype(jnp.bfloat16)
    returned_terms = lax.ppermute(partner_terms, "frame", swap)
    grad_pairs = grad_pairs_terms[:, :frame_count] + returned_terms.astype(jnp.float32)
    grad_projected = (
        jnp.concatenate([grad_query, grad_pairs], axis=2)
        .reshape(row_count, 3 * model_width)
        .astype(jnp.bfloat16)
    )
    grad_in_term = jnp.dot(hidden_first.T, grad_projected, preferred_element_type=jnp.float32)
    projected_sums = jnp.sum(grad_projected.astype(jnp.float32), axis=0)
    grad_query_bias = projected_sums[:model_width]
    grad_value_bias = projected_sums[2 * model_width :]
    grad_hidden_first = jnp.dot(grad_projected, full_in.T, preferred_element_type=jnp.float32)
    norm_term_first, gain_first, shift_first = norm_backward(
        grad_hidden_first, plain_first, inv_first, column_set[:, 0]
    )
    grad_inputs = (grad_residual + norm_term_first).astype(jnp.bfloat16).reshape(inputs.shape)
    grad_columns = jnp.stack(
        [
            gain_first,
            shift_first,
            grad_query_bias,
            grad_value_bias,
            grad_out_bias,
            gain_second,
            shift_second,
            grad_down_bias,
        ],
        axis=1,
    )
    small_grads = jnp.concatenate(
        [
            grad_columns,
            grad_bias_term.reshape(model_width, -1),
            jnp.zeros((model_width, 256 - 12), jnp.float32),
        ],
        axis=1,
    )
    first_terms, owned_late = lax.optimization_barrier(
        (jnp.concatenate([grad_in_term, small_grads], axis=1), owned_late)
    )
    owned_first = lax.psum_scatter(first_terms, everyone, scatter_dimension=0, tiled=True)
    owned_in = owned_first[:, :wide_in]
    owned_vectors = owned_first[:, wide_in : wide_in + vectors.shape[1]]
    owned_bias = owned_first[:, wide_in + vectors.shape[1] : wide_in + 12].reshape(-1)
    owned_shrink = owned_late[:, :ff_width].reshape(shrink_weight.shape)
    owned_expand = owned_late[:, ff_width : 2 * ff_width]
    owned_out = owned_late[:, 2 * ff_width :]
    new_in, mom_in = adam_step(project_in, moments_in, owned_in)
    new_out, mom_out = adam_step(project_out, moments_out, owned_out)
    new_expand, mom_expand = adam_step(expand_weight, moments_expand, owned_expand)
    new_shrink, mom_shrink = adam_step(shrink_weight, moments_shrink, owned_shrink)
    new_bias, mom_bias = adam_step(expand_bias, moments_bias, owned_bias)
    new_vectors, mom_vectors = adam_step(vectors, moments_vectors, owned_vectors)
    return (
        output,
        grad_inputs,
        owned_in,
        owned_out,
        owned_expand,
        owned_shrink,
        owned_bias,
        owned_vectors,
        new_in,
        new_out,
        new_expand,
        new_shrink,
        new_bias,
        new_vectors,
        mom_in,
        mom_out,
        mom_expand,
        mom_shrink,
        mom_bias,
        mom_vectors,
    )


def solution(mesh):
    in_specs = (
        P("clip", "frame", None),
        P("clip", "frame", None),
        P(("clip", "frame"), None),
        P(("clip", "frame"), None),
        P(("clip", "frame"), None),
        P(("clip", "frame"), None),
        P(("clip", "frame")),
        P(("clip", "frame"), None),
        P(None, ("clip", "frame"), None),
        P(None, ("clip", "frame"), None),
        P(None, ("clip", "frame"), None),
        P(None, ("clip", "frame"), None),
        P(None, ("clip", "frame")),
        P(None, ("clip", "frame"), None),
    )
    out_specs = (
        P("clip", "frame", None),
        P("clip", "frame", None),
        P(("clip", "frame"), None),
        P(("clip", "frame"), None),
        P(("clip", "frame"), None),
        P(("clip", "frame"), None),
        P(("clip", "frame")),
        P(("clip", "frame"), None),
        P(("clip", "frame"), None),
        P(("clip", "frame"), None),
        P(("clip", "frame"), None),
        P(("clip", "frame"), None),
        P(("clip", "frame")),
        P(("clip", "frame"), None),
        P(None, ("clip", "frame"), None),
        P(None, ("clip", "frame"), None),
        P(None, ("clip", "frame"), None),
        P(None, ("clip", "frame"), None),
        P(None, ("clip", "frame")),
        P(None, ("clip", "frame"), None),
    )
    return jax.shard_map(body, mesh=mesh, in_specs=in_specs, out_specs=out_specs, check_vma=False)
```

profile of v0, /device:TPU:0, one launch (start us, length us, event | category | flops | bytes accessed | tf_op | source)
XLA Modules:
  0.0 796.1 jit_solution(1115466514428548295)
XLA Ops:
  14.4 60.6 %all-gather.3.cloned.1.call-done = bf16[768,2432]{1,0:T(8,128)(2,1)} async-done(((bf16[24,2432]{1,0:T(8,128)(2,1)}), bf16[768,2432]{1,0:T(8,128)(2,1)}) %all-gather.3.cloned.1.call-update) | async-done | bytes 3735568 | tf_op jit(solution)/shard_map/all_gather | solution.py:179
  81.1 5.1 add_convert_fusion
  89.6 18.6 %collective-permute-done = bf16[750,768]{1,0:T(8,128)(2,1)} collective-permute-done((bf16[750,768]{1,0:T(8,128)(2,1)S(1)}, bf16[750,768]{1,0:T(8,128)(2,1)}, u32[]{:S(2)}, u32[]{:S(2)}) %collective-permute-start) | collective-permute-done | bytes 1152032 | tf_op jit(solution)/shard_map/ppermute | solution.py:195
  116.1 126.1 %while.30 = (s32[]{:T(128)}, bf16[12,1,750,64]{2,3,1,0:T(8,128)(2,1)}, f32[12,1,750]{2,1,0:T(1,128)S(1)}, s32[12]{0:T(128)S(1)}, bf16[1,750,768]{2,1,0:T(8,128)(...) while((s32[]{:T(128)}, ...), condition=%wide.region_5.6_spmd, body=%wide.region_2.5_spmd.sunk | while | flops 298124256 | bytes 32810912 | solution.py:74
  122.3 4.2 fusion.160
  132.8 4.4 fusion.160
  143.5 4.3 fusion.160
  154.0 4.5 fusion.160
  164.7 4.4 fusion.160
  175.3 4.2 fusion.160
  185.8 4.2 fusion.160
  196.2 4.2 fusion.160
  206.7 4.2 fusion.160
  217.1 4.2 fusion.160
  227.6 4.2 fusion.160
  238.0 4.2 fusion.160
  246.6 4.8 slice.186
  251.4 8.6 %reshape.414 = bf16[3072,768]{1,0:T(8,128)(2,1)} reshape(bf16[768,3072]{1,0:T(8,128)(2,1)} %slice.186) | data formatting | bytes 9437184 | tf_op jit(solution)/shard_map/reshape | solution.py:189
  260.0 7.1 multiply_convert_fusion.1
  267.1 7.6 convert_reduce_fusion
  274.7 7.0 fusion.127
  281.7 6.7 multiply_reduce_fusion.2
  292.2 6.6 fusion.88
  298.8 11.4 %reshape.423 = f32[768,3072]{1,0:T(8,128)} reshape(f32[3072,768]{1,0:T(8,128)} %fusion.88) | data formatting | bytes 18874368 | tf_op jit(solution)/shard_map/reshape | solution.py:243
  310.3 15.0 %pad_maximum_fusion = f32[768,6912]{1,0:T(8,128)} fusion(f32[768,768]{1,0:T(8,128)} %fusion.124, f32[768,3072]{1,0:T(8,128)} %fusion.127, f32[768,3072]{1,0:T(8,128)} %reshape.423), kind=kLoop, calls=%fused_computation.52 | loop fusion | flops 10616832 | bytes 42467328 | tf_op jit(solution)/shard_map/concatenate | solution.py:242
  330.6 231.7 %while.31 = (s32[]{:T(128)}, bf16[12,1,750,64]{2,3,1,0:T(8,128)(2,1)}, f32[12,1,1500,64]{2,3,1,0:T(8,128)}, f32[12,1,1500,64]{2,3,1,0:T(8,128)}, s32[12]{0:T(128...) while((s32[]{:T(128)}, ...), condition=%wide.region_12.13_spmd, body=%wide.region_10.12_spmd.sunk | while | flops 729143232 | bytes 50654712 | solution.py:118
  331.8 4.2 fusion.169
  338.0 4.5 multiply_reduce_fusion.10
  351.7 4.2 fusion.169
  357.9 4.5 multiply_reduce_fusion.10
  371.8 4.2 fusion.169
  410.0 4.1 fusion.169
  416.2 4.3 multiply_reduce_fusion.10
  429.4 4.1 fusion.169
  454.7 4.2 multiply_reduce_fusion.10
  467.9 4.1 fusion.169
  487.0 4.1 fusion.169
  506.2 4.1 fusion.169
  544.5 4.1 fusion.169
  562.3 5.0 fusion.49
  567.3 4.4 copy.80
  578.5 45.8 %collective-permute-done.1 = bf16[1,750,1536]{2,1,0:T(8,128)(2,1)} collective-permute-done((bf16[1,750,1536]{2,1,0:T(8,128)(2,1)}, bf16[1,750,1536]{2,1,0:T(8,128)(2,1)}, u32[]{:S(2)}, u32[]{:S(2)}) %collective-permute-start.1) | collective-permute-done | bytes 2304032 | tf_op jit(solution)/shard_map/ppermute | solution.py:257
  624.3 4.5 copy.81
  633.4 4.8 fusion.77
  642.5 6.3 fusion.54
  649.7 10.7 %concatenate.50 = f32[768,2560]{1,0:T(8,128)} concatenate(f32[768,2304]{1,0:T(8,128)} %fusion.54, f32[768,1]{1,0:T(8,128)} %stack.92, f32[768,1]{1,0:T(8,128)} %stack.93, f32[768,1]{1,0:T(8,128)} %stack.94, f32[768,1]{1,0:T(8,128)} %stack.95, f32[768,1]{1,0:T(8,128)} %stack.96, f32[768,1]{1,0:T(8,128)} %stack.97, f32[768,1]{1,0:T(8,128)} %stack.98, f32[768,1]{1,0:T(8,128)} %stack.99, ...), dimensions={1} | concatenate | bytes 15728640 | tf_op jit(solution)/shard_map/concatenate | solution.py:295
  661.4 8.8 %fusion.84 = bf16[1,750,768]{2,1,0:T(8,128)(2,1)} fusion(f32[750,768]{1,0:T(8,128)S(1)} %get-tuple-element.381, bf16[750,3072]{1,0:T(8,128)(2,1)} %copy-done.39, bf16[3072,768]{1,0:T(8,128)(2,1)} %reshape.414, f32[768]{0:T(1024)S(1)} %copy-done.35), kind=kOutput, calls=%fused_computation.124 | convolution fusion | flops 3540672000 | bytes 12785664 | tf_op jit(solution)/shard_map/dot_general | solution.py:222
  679.0 102.6 %reduce-scatter.5.cloned.1.call-done = f32[24,2560]{1,0:T(8,128)} async-done(((f32[768,2560]{1,0:T(8,128)}), f32[24,2560]{1,0:T(8,128)}) %reduce-scatter.5.cloned.1.call-update) | async-done | bytes 245776 | tf_op jit(solution)/shard_map/reduce_scatter | solution.py:297
  (407 shorter events, 282.5 us)
Async XLA Ops:
  7.2 6.4 copy-start.1
  7.2 67.7 %all-gather.3.cloned.1.call-start = ((), (), s32[]{:S(2)}) async-start(), calls=%async_computation.2 | async-start | bytes 3852288 | tf_op jit(solution)/shard_map/all_gather | solution.py:179
  10.6 231.7 %all-gather.5.cloned.1.call-start = ((), (), s32[]{:S(2)}) async-start(), calls=%async_computation.3 | async-start | bytes 10948608 | tf_op jit(solution)/shard_map/all_gather | solution.py:180
  13.9 63.7 %copy-start.24 = (f32[750]{0:T(1024)}, f32[750]{0:T(1024)S(1)}, u32[]{:S(2)}) copy-start(f32[750]{0:T(1024)S(1)} %broadcast_multiply_fusion.5) | copy-start | bytes 9004
  14.4 63.7 %copy-start.28 = (f32[750]{0:T(1024)}, f32[750]{0:T(1024)S(1)}, u32[]{:S(2)}) copy-start(f32[750]{0:T(1024)S(1)} %add_rsqrt_fusion.1) | copy-start | bytes 9004
  77.5 8.7 %copy-start.26 = (f32[768]{0:T(1024)}, f32[768]{0:T(1024)S(1)}, u32[]{:S(2)}) copy-start(f32[768]{0:T(1024)S(1)} %get-tuple-element.317) | copy-start | bytes 9220
  78.0 30.2 %collective-permute-start = (bf16[750,768]{1,0:T(8,128)(2,1)S(1)}, bf16[750,768]{1,0:T(8,128)(2,1)}, u32[]{:S(2)}, u32[]{:S(2)}) collective-permute-start(bf16[750,768]{1,0:T(8,128)(2,1)S(1)} %fusion.71), channel_id=1, source_target_pairs={{0,1},{1,0},{2,3},{3,2},{4,5},{5,4},{6,7},{7,6},{8,9},{9,8},{10,11... | collective-permute-start | bytes 3456008 | tf_op jit(solution)/shard_map/ppermute | solution.py:195
  80.3 580.1 %reduce-scatter.3.cloned.1.call-start = ((), (), s32[]{:S(2)}) async-start(), calls=%async_computation.4 | async-start | bytes 21897216 | tf_op jit(solution)/shard_map/reduce_scatter | solution.py:241
  89.6 22.6 %slice-start.2 = ((bf16[750,2304]{1,0:T(8,128)(2,1)}), bf16[750,1536]{1,0:T(8,128)(2,1)S(1)}, s32[]{:S(2)}) async-start(bf16[750,2304]{1,0:T(8,128)(2,1)} %copy-done.5), calls=%async_computation.8 | async-start | bytes 4620288 | tf_op jit(solution)/shard_map/slice | solution.py:207
  260.0 7.1 copy-start.6
  260.0 7.1 copy-start.16
  267.1 25.1 %copy-start.39 = (bf16[750,3072]{1,0:T(8,128)(2,1)}, bf16[750,3072]{1,0:T(8,128)(2,1)S(1)}, u32[]{:S(2)}) copy-start(bf16[750,3072]{1,0:T(8,128)(2,1)S(1)} %get-tuple-element.386) | copy-start | bytes 13824004
  325.3 456.2 %reduce-scatter.5.cloned.1.call-start = ((), (), s32[]{:S(2)}) async-start(), calls=%async_computation.5 | async-start | bytes 8110080 | tf_op jit(solution)/shard_map/reduce_scatter | solution.py:297
  338.0 4.7 slice-start
  338.0 4.8 slice-start.1
  357.9 4.7 slice-start
  357.9 4.8 slice-start.1
  377.9 4.1 slice-start
  377.9 4.0 slice-start.1
  397.0 4.1 slice-start
  397.0 4.1 slice-start.1
  416.1 4.3 slice-start
  416.2 4.4 slice-start.1
  435.5 4.1 slice-start
  435.6 4.1 slice-start.1
  454.7 4.2 slice-start
  454.7 4.3 slice-start.1
  474.0 4.1 slice-start
  474.0 4.0 slice-start.1
  493.1 4.1 slice-start
  493.1 4.1 slice-start.1
  512.3 4.1 slice-start
  512.3 4.1 slice-start.1
  531.4 4.1 slice-start
  531.4 4.1 slice-start.1
  571.7 52.6 %collective-permute-start.1 = (bf16[1,750,1536]{2,1,0:T(8,128)(2,1)}, bf16[1,750,1536]{2,1,0:T(8,128)(2,1)}, u32[]{:S(2)}, u32[]{:S(2)}) collective-permute-start(bf16[1,750,1536]{2,1,0:T(8,128)(2,1)} %copy.80), channel_id=1, source_target_pairs={{0,1},{1,0},{2,3},{3,2},{4,5},{5,4},{6,7},{7,6},{8,9},{9,8},{10,11... | collective-permute-start | bytes 6912008 | tf_op jit(solution)/shard_map/ppermute | solution.py:257
  628.9 4.5 copy-start.33
  661.4 8.8 %copy-start.4 = (f32[750,768]{1,0:T(8,128)S(1)}, f32[750,768]{1,0:T(8,128)}, u32[]{:S(2)}) copy-start(f32[750,768]{1,0:T(8,128)} %copy-done.3) | copy-start | bytes 6912004
  661.4 8.8 %copy-start.9 = (f32[750,768]{1,0:T(8,128)S(1)}, f32[750,768]{1,0:T(8,128)}, u32[]{:S(2)}) copy-start(f32[750,768]{1,0:T(8,128)} %get-tuple-element.383) | copy-start | bytes 6912004
  672.1 5.0 copy-start.11
  672.1 4.1 copy-start.14
  672.2 4.9 copy-start.15
  676.2 107.7 %copy-start.17 = (f32[2,24,2304]{2,1,0:T(8,128)S(1)}, f32[2,24,2304]{2,1,0:T(8,128)}, u32[]{:S(2)}) copy-start(f32[2,24,2304]{2,1,0:T(8,128)} %param.26) | copy-start | bytes 1327108
  677.1 107.8 %copy-start.19 = (f32[24,2304]{1,0:T(8,128)S(1)}, f32[24,2304]{1,0:T(8,128)}, u32[]{:S(2)}) copy-start(f32[24,2304]{1,0:T(8,128)} %param.20) | copy-start | bytes 663556
  677.1 109.3 %copy-start.36 = (f32[2,96]{1,0:T(2,128)S(1)}, f32[2,96]{1,0:T(2,128)}, u32[]{:S(2)}) copy-start(f32[2,96]{1,0:T(2,128)} %param.30) | copy-start | bytes 2308
  677.2 109.3 %copy-start.38 = (f32[96]{0:T(128)S(1)}, f32[96]{0:T(128)}, u32[]{:S(2)}) copy-start(f32[96]{0:T(128)} %param.24) | copy-start | bytes 1156
  782.4 6.7 copy-start.37
  784.9 4.2 copy-start.18
  (34 other events, 80.7 us)
Sparse Core Ops, SparseCore 0:
  11.5 63.4 all-gather.2
  80.5 87.9 all-gather.4
  325.4 219.8 reduce-scatter.2
  660.6 120.8 reduce-scatter.4
where the time goes:
time: 803 us; the launch traced here: 796 us
  matrix products  334 us (42%)
  waiting for transfers between devices  228 us (28%)
  local copies, waits for them, and re-layouts  109 us (14%)
  other arithmetic  66.2 us (8%)
  loops' own time  40.4 us (5%)
  between operations  14.9 us (2%)
    reduce_scatter x1, waiting for transfers between devices, body(): lax.psum_scatter(first_terms, everyone, scatter_dimension=0, tiled=True)  103 us
    all_gather x1, waiting for transfers between devices, body(): first_full = lax.all_gather(first_pack, everyone, axis=0, tiled=True)  60.6 us
    dot_general x12, matrix products, one_head(): jnp.einsum('cqk,ckd->cqd', weights_soft, value_block, preferred_element_t...  51.6 us
    dot_general x12, matrix products, one_head_back(): jnp.einsum('cqd,ckd->cqk', query_block, key_block, preferred_element_type...  50 us
    dot_general x12, matrix products, one_head_back(): jnp.einsum('cqd,ckd->cqk', grad_block, value_block, preferred_element_typ...  49.6 us
    ppermute x1, waiting for transfers between devices, body(): returned_terms = lax.ppermute(partner_terms, 'frame', swap)  45.8 us
    another operation x1, loops' own time, attend_backward(): pieces = lax.map(one_head_back, jnp.arange(head_count))  32.1 us
    dot_general x12, matrix products, one_head_back(): jnp.einsum('cqk,ckd->cqd', grad_scores, key_block, preferred_element_type...  30.7 us
  transfers between devices with their start and end apart: 6, of which 4 were waited for; matrix products, arithmetic and copies ran while one was open for 48% of the time, Pallas kernels for 0%

commit v1 on v0

--- a/solution.py
+++ b/solution.py
@@ -3,6 +3,7 @@
 import jax.numpy as jnp
 from jax import lax
 from jax.sharding import PartitionSpec as P
+from jax.lax import all_gather
 
 HEADS = 12
 ADAM_STEP = 4
@@ -176,8 +177,9 @@
     second_pack = jnp.concatenate(
         [project_out, expand_weight, shrink_weight.reshape(shard_rows, -1)], axis=1
     ).astype(jnp.bfloat16)
-    first_full = lax.all_gather(first_pack, everyone, axis=0, tiled=True)
-    second_full = lax.all_gather(second_pack, everyone, axis=0, tiled=True)
+    earlier = jnp.concatenate([first_pack, second_pack], axis=1)
+    before = all_gather(earlier, everyone, axis=0, tiled=True)
+    first_full, second_full = jnp.split(before, [first_pack.shape[1]], axis=1)
     full_in = first_full[:, :wide_in]
     small_full = first_full[:, wide_in:].astype(jnp.float32)
     column_set = small_full[:, : vectors.shape[1]]

time: 803 us -> 838 us (1.044)
  waiting for transfers between devices: 228 us -> 258 us
    all_gather x2 -> x1, waiting for transfers between devices: 60.6 us -> 106 us  [body(): before = all_gather(earlier, everyone, axis=0, tiled=True)]
    ppermute x1, waiting for transfers between devices: 18.6 us -> 4.34 us  [body(): hidden_partner = lax.ppermute(hidden_first, 'frame', swap)]
  transfers between devices with their start and end apart: 6 -> 5, of which waited for: 4 -> 4; matrix products, arithmetic and copies ran while one was open for 48% -> 35% of each run, Pallas kernels for 0% -> 0%
where the time goes in v1:
time: 838 us; the launch traced here: 826 us
  matrix products  335 us (40%)
  waiting for transfers between devices  258 us (31%)
  local copies, waits for them, and re-layouts  109 us (13%)
  other arithmetic  65.7 us (8%)
  loops' own time  40.6 us (5%)
  between operations  14.7 us (2%)
    all_gather x1, waiting for transfers between devices, body(): before = all_gather(earlier, everyone, axis=0, tiled=True)  106 us
    reduce_scatter x1, waiting for transfers between devices, body(): lax.psum_scatter(first_terms, everyone, scatter_dimension=0, tiled=True)  102 us
    dot_general x12, matrix products, one_head(): jnp.einsum('cqk,ckd->cqd', weights_soft, value_block, preferred_element_t...  50.8 us
    dot_general x12, matrix products, one_head_back(): jnp.einsum('cqd,ckd->cqk', query_block, key_block, preferred_element_type...  50.2 us
    dot_general x12, matrix products, one_head_back(): jnp.einsum('cqd,ckd->cqk', grad_block, value_block, preferred_element_typ...  48.9 us
    ppermute x1, waiting for transfers between devices, body(): returned_terms = lax.ppermute(partner_terms, 'frame', swap)  45.6 us
    another operation x1, loops' own time, attend_backward(): pieces = lax.map(one_head_back, jnp.arange(head_count))  32.1 us
    dot_general x12, matrix products, one_head_back(): jnp.einsum('cqk,ckd->cqd', grad_scores, key_block, preferred_element_type...  30.7 us
  transfers between devices with their start and end apart: 5, of which 4 were waited for; matrix products, arithmetic and copies ran while one was open for 35% of the time, Pallas kernels for 0%

profile of v1, /device:TPU:0, one launch (start us, length us, event | category | flops | bytes accessed | tf_op | source)
XLA Modules:
  0.0 826.1 jit_solution(16577361078320696941)
XLA Ops:
  14.5 106.1 %all-gather.2.cloned.1.call-done = bf16[768,9344]{1,0:T(8,128)(2,1)} async-done(((bf16[24,9344]{1,0:T(8,128)(2,1)}), bf16[768,9344]{1,0:T(8,128)(2,1)}) %all-gather.2.cloned.1.call-update) | async-done | bytes 14352400 | tf_op jit(solution)/shard_map/all_gather | solution.py:181
  125.5 5.1 add_convert_fusion
  132.6 4.8 slice.191
  137.4 8.5 %reshape.414 = bf16[3072,768]{1,0:T(8,128)(2,1)} reshape(bf16[768,3072]{1,0:T(8,128)(2,1)} %slice.191) | data formatting | bytes 9437184 | tf_op jit(solution)/shard_map/reshape | solution.py:191
  147.2 4.3 collective-permute-done
  159.4 126.5 %while.30 = (s32[]{:T(128)}, bf16[12,1,750,64]{2,3,1,0:T(8,128)(2,1)}, f32[12,1,750]{2,1,0:T(1,128)S(1)}, s32[12]{0:T(128)S(1)}, bf16[1,750,768]{2,1,0:T(8,128)(...) while((s32[]{:T(128)}, ...), condition=%wide.region_5.6_spmd, body=%wide.region_2.5_spmd.sunk | while | flops 298124256 | bytes 32810912 | solution.py:75
  165.7 4.2 fusion.160
  176.2 4.2 fusion.160
  186.7 4.2 fusion.160
  197.3 4.2 fusion.160
  207.8 4.2 fusion.160
  218.3 4.2 fusion.160
  228.9 4.2 fusion.160
  239.4 4.2 fusion.160
  249.9 4.2 fusion.160
  260.5 4.2 fusion.160
  271.0 4.2 fusion.160
  281.5 4.2 fusion.160
  290.3 7.2 multiply_convert_fusion.1
  297.6 7.6 convert_reduce_fusion
  305.2 7.0 fusion.127
  312.2 6.7 multiply_reduce_fusion.2
  323.1 6.4 fusion.88
  329.5 11.5 %reshape.423 = f32[768,3072]{1,0:T(8,128)} reshape(f32[3072,768]{1,0:T(8,128)} %fusion.88) | data formatting | bytes 18874368 | tf_op jit(solution)/shard_map/reshape | solution.py:245
  340.9 15.0 %pad_maximum_fusion = f32[768,6912]{1,0:T(8,128)} fusion(f32[768,768]{1,0:T(8,128)} %fusion.124, f32[768,3072]{1,0:T(8,128)} %fusion.127, f32[768,3072]{1,0:T(8,128)} %reshape.423), kind=kLoop, calls=%fused_computation.52 | loop fusion | flops 10616832 | bytes 42467328 | tf_op jit(solution)/shard_map/concatenate | solution.py:244
  356.0 4.1 fusion.83
  361.2 231.2 %while.31 = (s32[]{:T(128)}, bf16[12,1,750,64]{2,3,1,0:T(8,128)(2,1)}, f32[12,1,1500,64]{2,3,1,0:T(8,128)}, f32[12,1,1500,64]{2,3,1,0:T(8,128)}, s32[12]{0:T(128...) while((s32[]{:T(128)}, ...), condition=%wide.region_12.13_spmd, body=%wide.region_10.12_spmd.sunk | while | flops 729143232 | bytes 50654712 | solution.py:119
  362.5 4.1 fusion.169
  368.6 4.5 multiply_reduce_fusion.10
  382.4 4.1 fusion.169
  388.5 4.5 multiply_reduce_fusion.10
  402.3 4.1 fusion.169
  440.4 4.1 fusion.169
  446.5 4.3 multiply_reduce_fusion.10
  465.9 4.1 multiply_reduce_fusion.10
  484.9 4.3 multiply_reduce_fusion.10
  523.4 4.2 multiply_reduce_fusion.10
  536.5 4.1 fusion.169
  555.5 4.1 fusion.169
  592.4 5.0 fusion.49
  597.4 4.3 copy.80
  608.4 45.6 %collective-permute-done.1 = bf16[1,750,1536]{2,1,0:T(8,128)(2,1)} collective-permute-done((bf16[1,750,1536]{2,1,0:T(8,128)(2,1)}, bf16[1,750,1536]{2,1,0:T(8,128)(2,1)}, u32[]{:S(2)}, u32[]{:S(2)}) %collective-permute-start.1) | collective-permute-done | bytes 2304032 | tf_op jit(solution)/shard_map/ppermute | solution.py:259
  654.0 4.4 copy.81
  662.2 6.8 fusion.77
  673.3 6.3 fusion.54
  680.5 10.7 %concatenate.49 = f32[768,2560]{1,0:T(8,128)} concatenate(f32[768,2304]{1,0:T(8,128)} %fusion.54, f32[768,1]{1,0:T(8,128)} %stack.92, f32[768,1]{1,0:T(8,128)} %stack.93, f32[768,1]{1,0:T(8,128)} %stack.94, f32[768,1]{1,0:T(8,128)} %stack.95, f32[768,1]{1,0:T(8,128)} %stack.96, f32[768,1]{1,0:T(8,128)} %stack.97, f32[768,1]{1,0:T(8,128)} %stack.98, f32[768,1]{1,0:T(8,128)} %stack.99, ...), dimensions={1} | concatenate | bytes 15728640 | tf_op jit(solution)/shard_map/concatenate | solution.py:297
  692.1 8.8 %fusion.84 = bf16[1,750,768]{2,1,0:T(8,128)(2,1)} fusion(f32[750,768]{1,0:T(8,128)S(1)} %get-tuple-element.381, bf16[750,3072]{1,0:T(8,128)(2,1)} %copy-done.37, bf16[3072,768]{1,0:T(8,128)(2,1)} %reshape.414, f32[768]{0:T(1024)S(1)} %copy-done.33), kind=kOutput, calls=%fused_computation.124 | convolution fusion | flops 3540672000 | bytes 12785664 | tf_op jit(solution)/shard_map/dot_general | solution.py:224
  709.7 102.1 %reduce-scatter.5.cloned.1.call-done = f32[24,2560]{1,0:T(8,128)} async-done(((f32[768,2560]{1,0:T(8,128)}), f32[24,2560]{1,0:T(8,128)}) %reduce-scatter.5.cloned.1.call-update) | async-done | bytes 245776 | tf_op jit(solution)/shard_map/reduce_scatter | solution.py:299
  (404 shorter events, 281.2 us)
Async XLA Ops:
  7.2 6.5 copy-start.1
  7.2 113.4 %all-gather.2.cloned.1.call-start = ((), (), s32[]{:S(2)}) async-start(), calls=%async_computation.2 | async-start | bytes 14800896 | tf_op jit(solution)/shard_map/all_gather | solution.py:181
  13.7 677.6 %reduce-scatter.3.cloned.1.call-start = ((), (), s32[]{:S(2)}) async-start(), calls=%async_computation.3 | async-start | bytes 21897216 | tf_op jit(solution)/shard_map/reduce_scatter | solution.py:243
  14.0 109.3 %copy-start.23 = (f32[750]{0:T(1024)}, f32[750]{0:T(1024)S(1)}, u32[]{:S(2)}) copy-start(f32[750]{0:T(1024)S(1)} %broadcast_multiply_fusion.5) | copy-start | bytes 9004
  14.5 109.2 %copy-start.27 = (f32[750]{0:T(1024)}, f32[750]{0:T(1024)S(1)}, u32[]{:S(2)}) copy-start(f32[750]{0:T(1024)S(1)} %add_rsqrt_fusion.1) | copy-start | bytes 9004
  123.2 7.4 copy-start.29
  123.7 27.8 %collective-permute-start = (bf16[750,768]{1,0:T(8,128)(2,1)S(1)}, bf16[750,768]{1,0:T(8,128)(2,1)}, u32[]{:S(2)}, u32[]{:S(2)}) collective-permute-start(bf16[750,768]{1,0:T(8,128)(2,1)S(1)} %fusion.71), channel_id=1, source_target_pairs={{0,1},{1,0},{2,3},{3,2},{4,5},{5,4},{6,7},{7,6},{8,9},{9,8},{10,11... | collective-permute-start | bytes 3456008 | tf_op jit(solution)/shard_map/ppermute | solution.py:197
  147.2 8.3 %slice-start.2 = ((bf16[750,2304]{1,0:T(8,128)(2,1)}), bf16[750,1536]{1,0:T(8,128)(2,1)S(1)}, s32[]{:S(2)}) async-start(bf16[750,2304]{1,0:T(8,128)(2,1)} %copy-done.5), calls=%async_computation.7 | async-start | bytes 4620288 | tf_op jit(solution)/shard_map/slice | solution.py:209
  289.9 7.7 slice-start.3
  290.3 7.3 slice-start.4
  290.3 7.3 copy-start.15
  297.5 25.6 %copy-start.37 = (bf16[750,3072]{1,0:T(8,128)(2,1)}, bf16[750,3072]{1,0:T(8,128)(2,1)S(1)}, u32[]{:S(2)}) copy-start(bf16[750,3072]{1,0:T(8,128)(2,1)S(1)} %get-tuple-element.386) | copy-start | bytes 13824004
  356.0 455.9 %reduce-scatter.5.cloned.1.call-start = ((), (), s32[]{:S(2)}) async-start(), calls=%async_computation.4 | async-start | bytes 8110080 | tf_op jit(solution)/shard_map/reduce_scatter | solution.py:299
  368.6 4.7 slice-start
  368.6 4.8 slice-start.1
  388.5 4.7 slice-start
  388.5 4.8 slice-start.1
  408.4 4.1 slice-start
  408.4 4.0 slice-start.1
  427.4 4.1 slice-start
  427.4 4.1 slice-start.1
  446.5 4.3 slice-start
  446.5 4.3 slice-start.1
  465.8 4.1 slice-start
  465.8 4.1 slice-start.1
  484.9 4.3 slice-start
  484.9 4.3 slice-start.1
  504.3 4.1 slice-start
  504.3 4.1 slice-start.1
  523.3 4.2 slice-start
  523.3 4.2 slice-start.1
  542.5 4.1 slice-start
  542.5 4.0 slice-start.1
  561.6 4.1 slice-start
  561.6 4.1 slice-start.1
  580.7 4.0 slice-start
  601.8 52.2 %collective-permute-start.1 = (bf16[1,750,1536]{2,1,0:T(8,128)(2,1)}, bf16[1,750,1536]{2,1,0:T(8,128)(2,1)}, u32[]{:S(2)}, u32[]{:S(2)}) collective-permute-start(bf16[1,750,1536]{2,1,0:T(8,128)(2,1)} %copy.80), channel_id=1, source_target_pairs={{0,1},{1,0},{2,3},{3,2},{4,5},{5,4},{6,7},{7,6},{8,9},{9,8},{10,11... | collective-permute-start | bytes 6912008 | tf_op jit(solution)/shard_map/ppermute | solution.py:259
  692.1 8.8 %copy-start.4 = (f32[750,768]{1,0:T(8,128)S(1)}, f32[750,768]{1,0:T(8,128)}, u32[]{:S(2)}) copy-start(f32[750,768]{1,0:T(8,128)} %copy-done.3) | copy-start | bytes 6912004
  692.1 8.8 %copy-start.8 = (f32[750,768]{1,0:T(8,128)S(1)}, f32[750,768]{1,0:T(8,128)}, u32[]{:S(2)}) copy-start(f32[750,768]{1,0:T(8,128)} %get-tuple-element.383) | copy-start | bytes 6912004
  702.9 5.0 copy-start.10
  702.9 4.1 copy-start.13
  703.0 4.9 copy-start.14
  707.0 107.3 %copy-start.16 = (f32[2,24,2304]{2,1,0:T(8,128)S(1)}, f32[2,24,2304]{2,1,0:T(8,128)}, u32[]{:S(2)}) copy-start(f32[2,24,2304]{2,1,0:T(8,128)} %param.26) | copy-start | bytes 1327108
  707.9 107.3 %copy-start.18 = (f32[24,2304]{1,0:T(8,128)S(1)}, f32[24,2304]{1,0:T(8,128)}, u32[]{:S(2)}) copy-start(f32[24,2304]{1,0:T(8,128)} %param.20) | copy-start | bytes 663556
  707.9 108.8 %copy-start.34 = (f32[2,96]{1,0:T(2,128)S(1)}, f32[2,96]{1,0:T(2,128)}, u32[]{:S(2)}) copy-start(f32[2,96]{1,0:T(2,128)} %param.30) | copy-start | bytes 2308
  707.9 108.8 %copy-start.36 = (f32[96]{0:T(128)S(1)}, f32[96]{0:T(128)}, u32[]{:S(2)}) copy-start(f32[96]{0:T(128)} %param.24) | copy-start | bytes 1156
  812.7 6.7 copy-start.35
  815.2 4.2 copy-start.17
  (33 other events, 76.3 us)
Sparse Core Ops, SparseCore 0:
  13.8 106.7 all-gather.1
  356.1 217.9 reduce-scatter.2
  691.4 120.3 reduce-scatter.4
